TPU v7x, 32 devices: a whole 2x2x4 slice. The times are simulated.
32 devices in a mesh: groups: 2 (over y), seq: 4 (over z), mp: 2 (over x), rep: 2 (over core).
Axes of the slice: x: 2, y: 2, z: 4, core: 2. Of those that a mesh axis runs over, the one named last changes fastest.
Arguments:
- tokens: bfloat16 [8192, 2240], P(('groups', 'seq', 'rep')), parts along dimension 0, may hold values from -8 to 8
- slot_image: int32 [32], P(('groups', 'seq', 'rep')), parts along dimension 0, may hold values from 0 to 5, as said below
- modulation: float32 [12, 3, 2240], P('groups'), parts along dimension 0, may hold values from -3 to 3
- w_qkv: bfloat16 [2240, 3, 1280], P('rep', None, 'mp'), may hold values from -0.125 to 0.125
- w_out: bfloat16 [1280, 2240], P('rep', 'mp'), may hold values from -0.15625 to 0.15625
Outputs:
- updated: bfloat16 [8192, 2240], P(('groups', 'seq', 'rep'), 'mp'), parts along dimension 0
There are 2 independent parts, one for each index of `groups`. A program takes and returns all parts, laid end to end along the dimension named above; an argument that names none is the same for every part. Nothing has to cross between parts.
Inputs may be any that keep to these rules, and one draw needn't show every extreme that they name: `slot_image`: every one of the 6 images owns one tile slot or more.
All inputs are finite; a program needn't handle non-finite values.
Results may differ from a plain program's by a relative error of at most 0.0036.
Values may be sent and summed in bfloat16 or wider, within the bound.
No kernel may reach another device: no remote copies, remote signals or barrier semaphores. Data moves between devices by JAX's collectives and lax.ppermute only.
A program may use at most 128 MiB of HBM per device.

v0:
```python
import jax
import jax.numpy as jnp
from jax import lax
from jax.sharding import PartitionSpec as P

D = 2240
HD = 32


def body(tokens, slot_image, modulation, w_qkv, w_out):
    hi = lax.Precision.HIGHEST
    tiles = slot_image.shape[0]
    rows = tokens.shape[0]
    tile_len = rows // tiles
    images = modulation.shape[0]
    width = w_qkv.shape[2]
    per_dev = width // HD
    picker = (slot_image[:, None] == jnp.arange(images, dtype=jnp.int32)[None, :]).astype(
        jnp.float32
    )
    per_tile = jnp.dot(picker, modulation.reshape(images, 3 * D), precision=hi).reshape(tiles, 3, D)
    xf = tokens.astype(jnp.float32).reshape(tiles, tile_len, D)
    mean = jnp.mean(xf, axis=2, keepdims=True)
    var = jnp.mean((xf - mean) ** 2, axis=2, keepdims=True)
    normed = (xf - mean) / jnp.sqrt(var + 1e-06)
    modulated = (normed * (1.0 + per_tile[:, None, 1, :]) + per_tile[:, None, 0, :]).astype(
        jnp.bfloat16
    )
    modulated = modulated.reshape(rows, D)
    qkv = jnp.einsum(
        "td,dcm->tcm",
        modulated,
        lax.all_gather(w_qkv, "rep", axis=0, tiled=True),
        preferred_element_type=jnp.float32,
    )
    qkv = qkv.reshape(tiles, tile_len, 3, per_dev, HD)
    query = jax.nn.relu(qkv[:, :, 0]).astype(jnp.bfloat16)
    keyf = jax.nn.relu(qkv[:, :, 1]).astype(jnp.bfloat16)
    value = qkv[:, :, 2].astype(jnp.bfloat16)
    tile_state = jnp.einsum("slhe,slhf->shef", keyf, value, preferred_element_type=jnp.float32)
    tile_ksum = jnp.sum(keyf.astype(jnp.float32), axis=1)
    state = jnp.einsum("si,shef->ihef", picker, tile_state, precision=hi)
    ksum = jnp.einsum("si,she->ihe", picker, tile_ksum, precision=hi)
    state, ksum = lax.psum((state, ksum), ("seq", "rep"))
    own_state = jnp.einsum("si,ihef->shef", picker, state, precision=hi)
    own_ksum = jnp.einsum("si,ihe->she", picker, ksum, precision=hi)
    query_wide = query.astype(jnp.float32)
    numer = jnp.einsum("slhe,shef->slhf", query_wide, own_state, precision=hi)
    denom = jnp.einsum("slhe,she->slh", query_wide, own_ksum, precision=hi) + 1e-06
    attn = (numer / denom[..., None]).astype(jnp.bfloat16).reshape(rows, per_dev * HD)
    out_full = lax.all_gather(w_out, "rep", axis=0, tiled=True)
    cols = out_full.shape[1]
    projected = jnp.dot(
        lax.all_gather(attn, "mp", axis=1, tiled=True), out_full, preferred_element_type=jnp.float32
    )
    offset = lax.axis_index("mp") * cols
    own_tokens = (
        lax.dynamic_slice_in_dim(tokens, offset, cols, 1)
        .astype(jnp.float32)
        .reshape(tiles, tile_len, cols)
    )
    gate = lax.dynamic_slice_in_dim(per_tile[:, 2, :], offset, cols, 1)
    updated = own_tokens + gate[:, None, :] * projected.reshape(tiles, tile_len, cols)
    return updated.astype(jnp.bfloat16).reshape(rows, cols)


def solution(mesh):
    return jax.shard_map(
        body,
        mesh=mesh,
        in_specs=(
            P(("groups", "seq", "rep"), None),
            P(("groups", "seq", "rep")),
            P("groups", None, None),
            P("rep", None, "mp"),
            P("rep", "mp"),
        ),
        out_specs=P(("groups", "seq", "rep"), "mp"),
        check_vma=False,
    )
```

profile of v0, /device:TPU:0, one launch (start us, length us, event | category | flops | bytes accessed | tf_op | source)
XLA Modules:
  0.0 175.1 jit_solution(10275999285317942195)
XLA Ops:
  6.5 0.7 all-gather.4.cloned.1.call-update
  8.5 2.7 %mul.34 = f32[2,256,2240]{1,0,2:T(2,128)S(1)} broadcast(f32[2,2240]{0,1:T(8,128)S(1)} %copy.12), dimensions={0,2} | broadcast | bytes 4605440 | tf_op jit(solution)/shard_map/mul | solution.py:26
  11.3 2.6 %copy.34 = f32[280,8,2,256]{3,1,2,0:T(8,128)} copy(f32[280,8,2,256]{3,2,1,0:T(2,128)S(1)} %bitcast.80) | data formatting | bytes 9175040
  14.2 2.7 %add.57 = f32[2,256,2240]{1,0,2:T(2,128)S(1)} broadcast(f32[2,2240]{0,1:T(8,128)S(1)} %copy.13), dimensions={0,2} | broadcast | bytes 4605440 | tf_op jit(solution)/shard_map/add | solution.py:26
  17.5 1.5 copy-done
  20.1 3.0 %fusion.5 = bf16[512,2240]{0,1:T(8,128)(2,1)} fusion(f32[512,2240]{0,1:T(8,128)S(1)} %bitcast.79, f32[512,2240]{0,1:T(8,128)S(1)} %bitcast.78, bf16[512,2240]{0,1:T(8,128)(2,1)S(1)} %copy-done, f32[512]{0:T(512)S(1)} %add_sqrt_fusion, f32[512]{0:T(512)S(1)} %broadcast_multiply_fusion), kind=kLoop, calls=%fused_computation.7 | loop fusion | flops 6881280 | bytes 13766656 | tf_op jit(solution)/shard_map/convert_element_type | solution.py:26
  23.1 6.1 %dot_general.43 = bf16[2,256,2240]{1,0,2:T(2,128)(2,1)} reshape(bf16[512,2240]{0,1:T(8,128)(2,1)} %fusion.5) | data formatting | bytes 4587520 | tf_op jit(solution)/shard_map/td,dcm->tcm/dot_general | solution.py:30
  29.2 1.7 all-gather.4.cloned.1.call-done
  30.9 13.2 %copy.14 = bf16[3,640,2240]{2,1,0:T(8,128)(2,1)} copy(bf16[3,640,2240]{1,2,0:T(8,128)(2,1)} %bitcast.84) | data formatting | bytes 17203200 | tf_op jit(solution)/shard_map/td,dcm->tcm/dot_general | solution.py:30
  44.1 8.9 %fusion.10 = bf16[2,256,3,20,32]{1,4,3,2,0:T(8,128)(2,1)S(1)} fusion(bf16[3,20,32,2240,1]{3,2,1,0,4:T(8,128)(2,1)} %bitcast.83, bf16[2,256,2240,1,1]{1,0,2,4,3:T(2,128)(2,1)} %bitcast.88), kind=kOutput, calls=%fused_computation.13 | convolution fusion | flops 4404019200 | bytes 12861440 | tf_op jit(solution)/shard_map/td,dcm->tcm/dot_general | solution.py:30
  53.4 1.9 %fusion.22 = f32[6,20,32,32]{3,0,2,1:T(8,128)S(1)} fusion(f32[2,20,32,32]{3,2,1,0:T(8,128)S(1)} %fusion.18, s32[2]{0:T(128)S(1)} %copy-done.3), kind=kOutput, calls=%fused_computation.30 | convolution fusion | flops 2949132 | bytes 655368 | tf_op jit(solution)/shard_map/si,shef->ihef/dot_general | solution.py:42
  55.4 1.7 copy.20
  57.9 1.3 convert_reduce_fusion.1
  59.6 31.6 %psum.15 = f32[6,20,32]{2,1,0:T(8,128)S(1)} all-reduce(f32[6,20,32]{2,1,0:T(8,128)S(1)} %copy.24), channel_id=1, replica_groups=mesh['groups'=2,'seq'=4,'mp'=2,'rep'=2] {'seq','rep'}, use_global_device_ids=true, to_apply=%region_4.5 | all-reduce | flops 3840 | bytes 30720 | tf_op jit(solution)/shard_map/psum | solution.py:44
  91.4 1.5 fusion.27
  92.9 30.4 %all-reduce.2.cloned.1.call-done = f32[6,20,32,32]{3,2,1,0:T(8,128)} async-done(((f32[6,20,32,32]{3,2,1,0:T(8,128)}), f32[6,20,32,32]{3,2,1,0:T(8,128)}) %all-reduce.2.cloned.1.call-update) | async-done | bytes 491536 | tf_op jit(solution)/shard_map/psum | solution.py:44
  123.3 3.9 %fusion.8 = f32[2,20,32,32]{3,0,2,1:T(2,128)S(1)} fusion(f32[6,20,32,32]{3,2,1,0:T(8,128)} %all-reduce.2.cloned.1.call-done, s32[2]{0:T(128)S(1)} %copy-done.3), kind=kOutput, calls=%fused_computation.11 | convolution fusion | flops 2949132 | bytes 655368 | tf_op jit(solution)/shard_map/si,ihef->shef/dot_general | solution.py:45
  127.2 1.9 %fusion.13 = bf16[2,256,20,32]{1,3,2,0:T(8,128)(2,1)S(1)} fusion(f32[2,20,32,32]{3,0,2,1:T(2,128)S(1)} %fusion.8, f32[2,256,20]{1,2,0:T(8,128)S(1)} %fusion.31, bf16[2,256,3,20,32]{1,4,3,2,0:T(8,128)(2,1)} %copy-done.2), kind=kOutput, calls=%fused_computation.17 | convolution fusion | flops 127467520 | bytes 1515520 | tf_op jit(solution)/shard_map/slhe,shef->slhf/dot_general | solution.py:48
  129.8 0.9 copy.36
  131.1 1.3 mul.31
  132.5 1.6 copy.33
  134.1 2.0 %all-gather.8.cloned.1.call-done = bf16[1280,1120]{0,1:T(8,128)(2,1)} async-done(((bf16[640,1120]{0,1:T(8,128)(2,1)}), bf16[1280,1120]{0,1:T(8,128)(2,1)}) %all-gather.8.cloned.1.call-update) | async-done | bytes 2867216 | tf_op jit(solution)/shard_map/all_gather | solution.py:51
  136.1 26.8 %all-gather.6.cloned.1.call-done = bf16[512,1280]{0,1:T(8,128)(2,1)} async-done(((bf16[512,640]{0,1:T(8,128)(2,1)}), bf16[512,1280]{0,1:T(8,128)(2,1)}) %all-gather.6.cloned.1.call-update) | async-done | bytes 1310736 | tf_op jit(solution)/shard_map/all_gather | solution.py:54
  162.9 5.6 %fusion.7 = bf16[512,1120]{0,1:T(8,128)(2,1)} fusion(f32[512,1120]{0,1:T(8,128)} %bitcast.87, bf16[1280,1120]{0,1:T(8,128)(2,1)} %all-gather.8.cloned.1.call-done, bf16[512,1280]{0,1:T(8,128)(2,1)} %all-gather.6.cloned.1.call-done, bf16[512,2240]{0,1:T(8,128)(2,1)S(1)} %copy-done, s32[]{:T(128)S(6)} %select_n.4), kind=kOutput, calls=%fused_computation.10 | convolution fusion | flops 1470300160 | bytes 8765444 | tf_op jit(solution)/shard_map/dot_general | solution.py:53
  (38 shorter events, 5.8 us)
Async XLA Ops:
  6.5 0.9 copy-start.1
  6.5 24.4 %all-gather.4.cloned.1.call-start = ((), (), s32[]{:S(2)}) async-start(), calls=%async_computation | async-start | bytes 12902400 | tf_op jit(solution)/shard_map/all_gather | solution.py:33
  6.5 1.3 copy-start.3
  7.3 116.1 %all-reduce.2.cloned.1.call-start = ((), (), s32[]{:S(2)}) async-start(), calls=%async_computation.1 | async-start | bytes 3932160 | tf_op jit(solution)/shard_map/psum | solution.py:44
  14.2 5.9 %slice-start = ((s8[4587520]{0:T(1024)(128)(4,1)}), s8[4194304]{0:T(1024)(128)(4,1)S(1)}, s32[]{:S(2)}) async-start(s8[4587520]{0:T(1024)(128)(4,1)} %bitcast.76), calls=%async_computation.4 | async-start | bytes 8388608
  17.0 2.1 %copy-start = (bf16[512,2240]{0,1:T(8,128)(2,1)S(1)}, bf16[512,2240]{0,1:T(8,128)(2,1)}, u32[]{:S(2)}) copy-start(bf16[512,2240]{0,1:T(8,128)(2,1)} %param.5) | copy-start | bytes 6881284
  17.0 3.1 %slice-start.1 = ((s8[4587520]{0:T(1024)(128)(4,1)}), s8[393216]{0:T(1024)(128)(4,1)S(1)}, s32[]{:S(2)}) async-start(s8[4587520]{0:T(1024)(128)(4,1)} %bitcast.76), calls=%async_computation.5 | async-start | bytes 786432
  53.1 2.3 %copy-start.2 = (bf16[2,256,3,20,32]{1,4,3,2,0:T(8,128)(2,1)}, bf16[2,256,3,20,32]{1,4,3,2,0:T(8,128)(2,1)S(1)}, u32[]{:S(2)}) copy-start(bf16[2,256,3,20,32]{1,4,3,2,0:T(8,128)(2,1)S(1)} %fusion.10) | copy-start | bytes 5898244
  57.1 79.0 %all-gather.8.cloned.1.call-start = ((), (), s32[]{:S(2)}) async-start(), calls=%async_computation.3 | async-start | bytes 4300800 | tf_op jit(solution)/shard_map/all_gather | solution.py:51
  57.8 105.1 %all-gather.6.cloned.1.call-start = ((), (), s32[]{:S(2)}) async-start(), calls=%async_computation.2 | async-start | bytes 1966080 | tf_op jit(solution)/shard_map/all_gather | solution.py:54
Sparse Core Ops, SparseCore 0:
  8.9 21.9 all-gather.3
  57.2 66.0 all-reduce.1
  124.9 11.1 all-gather.7
  137.5 25.3 all-gather.5
where the time goes:
time: 176 us; the launch traced here: 175 us
  waiting for transfers between devices  62.4 us (35%)
  local copies, waits for them, and re-layouts  37.3 us (21%)
  blocking collectives  31.6 us (18%)
  matrix products  24.9 us (14%)
  between operations  13.3 us (8%)
  other arithmetic  5.39 us (3%)
    psum x1, blocking collectives, body(): state, ksum = lax.psum((state, ksum), ('seq', 'rep'))  31.6 us
    psum x1, waiting for transfers between devices, body(): state, ksum = lax.psum((state, ksum), ('seq', 'rep'))  30.4 us
    all_gather x1, waiting for transfers between devices, body(): lax.all_gather(attn, 'mp', axis=1, tiled=True)  26.8 us
    dot_general x2, local copies, waits for them, and re-layouts, body(): jnp.einsum('td,dcm->tcm', modulated, lax.all_gather(w_qkv, 'rep', axis=0,...  19.3 us
    dot_general x1, matrix products, body(): jnp.einsum('td,dcm->tcm', modulated, lax.all_gather(w_qkv, 'rep', axis=0,...  8.95 us
    unnamed x16, local copies, waits for them, and re-layouts  7.35 us
    dot_general x1, matrix products, body(): jnp.dot(lax.all_gather(attn, 'mp', axis=1, tiled=True), out_full, preferr...  5.59 us
    dot_general x1, matrix products, body(): own_state = jnp.einsum('si,ihef->shef', picker, state, precision=hi)  3.93 us
  transfers between devices with their start and end apart: 4, of which 4 were waited for; matrix products, arithmetic and copies ran while one was open for 19% of the time, Pallas kernels for 0%

commit v1 on v0

v1 whole, which is shorter than its diff:
```python
import functools

import jax
import jax.numpy as jnp
from jax import lax
from jax.experimental import pallas as pl
from jax.experimental.pallas import tpu as pltpu
from jax.sharding import PartitionSpec as P

HD = 32
F32 = jnp.float32
BF16 = jnp.bfloat16
VM = pl.BlockSpec(memory_space=pltpu.VMEM)
HB = pl.BlockSpec(memory_space=pltpu.HBM)
MIB = 1 << 20


def call(kernel, name, out_shape, in_specs, out_specs=None, scratch=(), vmem=16, flops=0, nbytes=0):
    if out_specs is None:
        out_specs = [VM] * len(out_shape) if isinstance(out_shape, list) else VM
    return pl.pallas_call(
        kernel,
        out_shape=out_shape,
        in_specs=in_specs,
        out_specs=out_specs,
        scratch_shapes=list(scratch),
        compiler_params=pltpu.CompilerParams(vmem_limit_bytes=vmem * MIB),
        cost_estimate=pl.CostEstimate(flops=flops, bytes_accessed=nbytes, transcendentals=0),
        name=name,
    )


def load_kernel(w_ref, kv_ref, sems):
    count = kv_ref.shape[0]
    copies = [
        pltpu.make_async_copy(w_ref.at[c + 1], kv_ref.at[c], sems.at[c]) for c in range(count)
    ]
    for copy in copies:
        copy.start()
    for copy in copies:
        copy.wait()


def first_kernel(
    img_ref, x_ref, mods_ref, w_ref, kv_ref, mod_ref, part_ref, wq_ref, x_scr, mods_scr, img_scr,
    own_scr, sems,
):
    mine = lax.axis_index("rep")
    rows, half = mod_ref.shape
    width_in = x_ref.shape[0]
    halves = width_in // half
    tiles = img_ref.shape[0]
    step = 128
    per_tile = rows // tiles
    steps = rows // step
    img_copy = pltpu.make_async_copy(img_ref, img_scr, sems.at[0])
    mods_copy = pltpu.make_async_copy(mods_ref, mods_scr, sems.at[1])
    wq_copy = pltpu.make_async_copy(w_ref.at[0], wq_ref, sems.at[2])
    x_copies = [
        pltpu.make_async_copy(
            x_ref.at[:, pl.ds(i * step, step)], x_scr.at[:, pl.ds(i * step, step)], sems.at[3 + i]
        )
        for i in range(steps)
    ]
    img_copy.start()
    mods_copy.start()
    for copy in x_copies:
        copy.start()
    wq_copy.start()
    img_copy.wait()
    mods_copy.wait()
    for i in range(steps):
        x_copies[i].wait()
        at = slice(i * step, (i + 1) * step)
        parts = [
            x_scr[h * half : (h + 1) * half, at].astype(F32).T for h in range(halves)
        ]
        mean = sum(jnp.sum(p, axis=1, keepdims=True) for p in parts) / width_in
        parts = [p - mean for p in parts]
        var = sum(jnp.sum(p * p, axis=1, keepdims=True) for p in parts) / width_in
        inv = 1.0 / jnp.sqrt(var + 1e-06)
        mods = mods_scr[img_scr[i * step // per_tile]]
        for h in range(halves):
            shift = mods[0:1, h * half : (h + 1) * half]
            scale = mods[1:2, h * half : (h + 1) * half]
            own_scr[h, at, :] = (parts[h] * inv * (1.0 + scale) + shift).astype(BF16)
    mod_ref[...] = own_scr[1 - mine]
    for c in range(kv_ref.shape[0]):
        part_ref[c + 1] = jnp.dot(own_scr[mine], kv_ref[c], preferred_element_type=F32)
    wq_copy.wait()
    part_ref[0] = jnp.dot(own_scr[mine], wq_ref[...], preferred_element_type=F32)


def head_blocks(width):
    return [(start, min(128, width - start)) for start in range(0, width, 128)]


def same_head(rows, cols):
    return (
        lax.broadcasted_iota(jnp.int32, (rows, cols), 0) // HD
        == lax.broadcasted_iota(jnp.int32, (rows, cols), 1) // HD
    )


def state_rows(tiles):
    return tiles * HD + 8


def second_kernel(img_ref, mod_ref, w_ref, part_ref, state_ref, k_scr, v_scr, img_scr, sem):
    rows, width = k_scr.shape
    tiles = img_ref.shape[0]
    per_tile = rows // tiles
    img_copy = pltpu.make_async_copy(img_ref, img_scr, sem)
    img_copy.start()
    mod = mod_ref[...]
    k_scr[...] = jnp.maximum(
        part_ref[1] + jnp.dot(mod, w_ref[0], preferred_element_type=F32), 0.0
    ).astype(BF16)
    v_scr[...] = (
        part_ref[2] + jnp.dot(mod, w_ref[1], preferred_element_type=F32)
    ).astype(BF16)
    img_copy.wait()
    sums, images = [], []
    for t in range(tiles):
        span = slice(t * per_tile, (t + 1) * per_tile)
        sums.append(jnp.sum(k_scr[span, :].astype(F32), axis=0, keepdims=True))
        images.append(jnp.full((1, width), img_scr[t].astype(F32), F32))
        for start, size in head_blocks(width):
            full = lax.dot_general(
                v_scr[span, start : start + size],
                k_scr[span, start : start + size],
                (((0,), (0,)), ((), ())),
                preferred_element_type=F32,
            )
            full = jnp.where(same_head(size, size), full, 0.0)
            state_ref[t * HD : (t + 1) * HD, start : start + size] = sum(
                full[j * HD : (j + 1) * HD, :] for j in range(size // HD)
            ).astype(BF16)
    state_ref[tiles * HD :, :] = tail_rows(sums, images).astype(BF16)


def tail_rows(sums, images):
    rest = [s - s.astype(BF16).astype(F32) for s in sums]
    rows = sums + rest + images
    rows.append(jnp.zeros((8 - len(rows), sums[0].shape[1]), F32))
    return jnp.concatenate(rows, axis=0)


def query_kernel(mod_ref, w_ref, part_ref, after_ref, q_ref):
    q_ref[...] = jnp.maximum(
        part_ref[0] + jnp.dot(mod_ref[...], w_ref[...], preferred_element_type=F32), 0.0
    ).astype(BF16)


def sum_kernel(*refs):
    blocks, wide_ref, out_ref = refs[:-2], refs[-2], refs[-1]
    width = out_ref.shape[1]
    tiles = (out_ref.shape[0] - 8) // HD
    want = blocks[0][tiles * HD :, :].astype(F32)[2 * tiles : 3 * tiles]
    totals = [jnp.zeros((HD, width), F32)] * tiles
    sums = [jnp.zeros((1, width), F32)] * tiles
    for ref in blocks:
        tail = ref[tiles * HD :, :].astype(F32)
        for s in range(tiles):
            state = ref[s * HD : (s + 1) * HD, :].astype(F32)
            ksum = tail[s : s + 1] + tail[tiles + s : tiles + s + 1]
            for t in range(tiles):
                keep = (tail[2 * tiles + s : 2 * tiles + s + 1] == want[t : t + 1]).astype(F32)
                totals[t] += keep * state
                sums[t] += keep * ksum
    for t in range(tiles):
        wide_ref[t * HD : (t + 1) * HD, :] = totals[t]
        out_ref[t * HD : (t + 1) * HD, :] = totals[t].astype(BF16)
    tail = tail_rows(sums, [])
    wide_ref[tiles * HD :, :] = tail
    out_ref[tiles * HD :, :] = tail.astype(BF16)


def attend(q_ref, state_ref, out_ref, tiles):
    rows, width = q_ref.shape
    per_tile = rows // tiles
    exact = state_ref.dtype == F32
    tail = state_ref[tiles * HD :, :].astype(F32)
    for t in range(tiles):
        span = slice(t * per_tile, (t + 1) * per_tile)
        for start, size in head_blocks(width):
            lanes = slice(start, start + size)
            mask = same_head(size, size)
            state = state_ref[t * HD : (t + 1) * HD, lanes].astype(F32)
            state = jnp.concatenate([state] * (size // HD), axis=0)
            parts = [jnp.where(mask, state, 0.0)]
            for row in (t, tiles + t):
                parts.append(jnp.where(mask, jnp.broadcast_to(tail[row : row + 1, lanes], (size, size)), 0.0))
            if exact:
                parts.append(parts[0] - parts[0].astype(BF16).astype(F32))
            left = jnp.concatenate(parts, axis=0).astype(BF16)
            both = lax.dot_general(
                left, q_ref[span, lanes], (((1,), (1,)), ((), ())), preferred_element_type=F32
            )
            numer = both[:size]
            if exact:
                numer += both[3 * size :]
            denom = both[size : 2 * size] + both[2 * size : 3 * size] + 1e-06
            out_ref[start : start + size, span] = (numer / denom).astype(BF16)


def fetch_weights(p, width, w_refs, w_scr, sem):
    mine = lax.axis_index("rep")
    subs = w_refs[0].shape[1] // width
    for source, ref in enumerate(w_refs):
        @pl.when((p // subs == mine) == (source == 0))
        def _():
            pltpu.make_async_copy(ref, w_scr, sem).start()

    def finish():
        pltpu.make_async_copy(w_refs[0], w_scr, sem).wait()
        weights = w_scr[...]
        chosen = weights[:, :width]
        for s in range(1, subs):
            chosen = jnp.where(p % subs == s, weights[:, s * width : (s + 1) * width], chosen)
        return chosen

    return finish


def fifth_kernel(
    img_ref, q_ref, state_ref, w0_ref, w1_ref, x_ref, mods_ref, base_ref, gate_ref,
    attn_scr, w_scr, x_scr, gates_scr, img_scr, sems,
):
    m = lax.axis_index("mp")
    cols, rows = base_ref.shape
    tiles = img_ref.shape[0]
    per_tile = rows // tiles
    finish = fetch_weights(m, q_ref.shape[1], (w0_ref, w1_ref), w_scr, sems.at[0])
    copies = [
        pltpu.make_async_copy(img_ref, img_scr, sems.at[1]),
        pltpu.make_async_copy(x_ref.at[pl.ds(m * cols, cols), :], x_scr, sems.at[2]),
        pltpu.make_async_copy(mods_ref, gates_scr, sems.at[3]),
    ]
    for copy in copies:
        copy.start()
    attend(q_ref, state_ref, attn_scr, tiles)
    weights = finish()
    for copy in copies:
        copy.wait()
    total = jnp.dot(weights, attn_scr[...], preferred_element_type=F32)
    for t in range(tiles):
        gates = gates_scr[img_scr[t]][2:3]
        gate = gates[:, :cols]
        for p in range(1, gates.shape[1] // cols):
            gate = jnp.where(m == p, gates[:, p * cols : (p + 1) * cols], gate)
        for start in range(0, cols, 128):
            size = min(128, cols - start)
            column = jnp.broadcast_to(gate[:, start : start + size], (128, size)).T
            gate_ref[start : start + size, t * 128 : (t + 1) * 128] = column
            for left in range(t * per_tile, (t + 1) * per_tile, 128):
                piece = (slice(start, start + size), slice(left, left + 128))
                base_ref[piece] = x_scr[piece].astype(F32) + column * total[piece]


def sixth_kernel(others, mp, tiles, *refs):
    q_refs, state_refs = refs[:others], refs[others : 2 * others]
    w0_ref, w1_ref, base_ref, gate_ref, out_ref, attn_scr, w_scr, sems = refs[2 * others :]
    m = lax.axis_index("mp")
    cols, rows = out_ref.shape
    per_tile = rows // tiles
    total = None
    for index in range(others):
        p = lax.rem(m + mp - 1 - index, mp)
        finish = fetch_weights(p, q_refs[index].shape[1], (w0_ref, w1_ref), w_scr, sems.at[index])
        attend(q_refs[index], state_refs[index], attn_scr, tiles)
        part = jnp.dot(finish(), attn_scr[...], preferred_element_type=F32)
        total = part if total is None else total + part
    for t in range(tiles):
        column = gate_ref[:, t * 128 : (t + 1) * 128]
        for left in range(t * per_tile, (t + 1) * per_tile, 128):
            piece = (slice(0, cols), slice(left, left + 128))
            out_ref[piece] = (base_ref[piece] + column * total[piece]).astype(BF16)


def body(tokens, slot_image, modulation, w_qkv, w_out, *, seq, mp):
    rows, depth = tokens.shape
    tiles = slot_image.shape[0]
    half, _, width = w_qkv.shape
    heads_half, cols = w_out.shape
    swap = [(0, 1), (1, 0)]
    shape = jax.ShapeDtypeStruct
    x = tokens.T
    w = jnp.transpose(w_qkv, (1, 0, 2))
    wo = w_out.T
    dma = pltpu.SemaphoreType.DMA
    images = modulation.shape[0]

    def shift(value, axis, size, by):
        return lax.ppermute(value, axis, [(i, (i + by) % size) for i in range(size)])

    def across(value):
        return lax.ppermute(value, "rep", swap)

    kv = call(load_kernel, "load", shape((2, half, width), BF16), [HB], scratch=[dma((2,))], vmem=54,
              nbytes=4 * half * width)(w)
    kv_theirs = across(kv)
    mod, part, wq = call(
        first_kernel, "first",
        [shape((rows, half), BF16), shape((3, rows, width), F32), shape((half, width), BF16)],
        [HB, HB, HB, HB, VM],
        scratch=[
            pltpu.VMEM((depth, rows), BF16), pltpu.VMEM(modulation.shape, F32), pltpu.SMEM((tiles,), jnp.int32),
            pltpu.VMEM((depth // half, rows, half), BF16), dma((3 + rows // 128,)),
        ],
        vmem=48, flops=2 * rows * half * 3 * width, nbytes=12 * MIB,
    )(slot_image, x, modulation, w, kv)
    wq_theirs = across(wq)
    block = (state_rows(tiles), width)
    state = call(
        second_kernel, "second", shape(block, BF16), [HB, VM, VM, VM],
        scratch=[pltpu.VMEM((rows, width), BF16)] * 2 + [pltpu.SMEM((tiles,), jnp.int32), dma],
        flops=2 * rows * half * 2 * width, nbytes=8 * MIB,
    )(slot_image, mod, kv_theirs, part)
    near = [state] + [shift(state, "seq", seq, d) for d in range(1, seq)]
    q = call(
        query_kernel, "query", shape((rows, width), BF16), [VM, VM, VM, VM],
        flops=2 * rows * half * width, nbytes=4 * MIB,
    )(mod, wq_theirs, part, state)
    q_theirs = [shift(q, "mp", mp, d) for d in range(1, mp)]
    wo_theirs = across(wo)
    far = [across(b) for b in near]
    wide, final = call(
        sum_kernel, "sum", [shape(block, F32), shape(block, BF16)], [VM] * (2 * seq), nbytes=MIB,
    )(*near, *far)
    finals = [shift(final, "mp", mp, d) for d in range(1, mp)]
    base, gate = call(
        fifth_kernel, "own", [shape((cols, rows), F32), shape((cols, tiles * 128), F32)],
        [HB, VM, VM, HB, HB, HB, HB],
        scratch=[
            pltpu.VMEM((width, rows), BF16), pltpu.VMEM((cols, heads_half), BF16), pltpu.VMEM((cols, rows), BF16),
            pltpu.VMEM(modulation.shape, F32), pltpu.SMEM((tiles,), jnp.int32), dma((4,)),
        ],
        flops=2 * rows * width * cols, nbytes=4 * MIB,
    )(slot_image, q, wide, wo, wo_theirs, x, modulation)
    out = call(
        functools.partial(sixth_kernel, mp - 1, mp, tiles), "others", shape((cols, rows), BF16),
        [VM] * (2 * (mp - 1)) + [HB, HB, VM, VM],
        scratch=[pltpu.VMEM((width, rows), BF16), pltpu.VMEM((cols, heads_half), BF16), dma((mp - 1,))],
        flops=2 * rows * width * cols, nbytes=4 * MIB,
    )(*q_theirs, *finals, wo, wo_theirs, base, gate)
    return out.T


def solution(mesh):
    sizes = dict(mesh.shape)
    return jax.shard_map(
        functools.partial(body, seq=sizes["seq"], mp=sizes["mp"]),
        mesh=mesh,
        in_specs=(
            P(("groups", "seq", "rep"), None),
            P(("groups", "seq", "rep")),
            P("groups", None, None),
            P("rep", None, "mp"),
            P("rep", "mp"),
        ),
        out_specs=P(("groups", "seq", "rep"), "mp"),
        check_vma=False,
    )
```

time: 176 us -> 45.2 us (0.26)
  waiting for transfers between devices: 62.4 us -> 7.73 us
  local copies, waits for them, and re-layouts: 37.3 us -> 2.13 us
  blocking collectives: 31.6 us -> 0 us
  matrix products: 24.9 us -> 0 us
  Pallas kernels: 0 us -> 24.7 us
  between operations: 13.3 us -> 0.08 us
  starting transfers between devices: 0.12 us -> 10.5 us
  other arithmetic: 5.39 us -> 0 us
    psum x1 -> x0, blocking collectives: 31.6 us -> none  [body(): state, ksum = lax.psum((state, ksum), ('seq', 'rep'))]
    all_gather x3 -> x0, waiting for transfers between devices: 30.6 us -> none  [the longest x1 26.8 us: body(): lax.all_gather(attn, 'mp', axis=1, tiled=True)]
    psum x1 -> x0, waiting for transfers between devices: 30.4 us -> none  [body(): state, ksum = lax.psum((state, ksum), ('seq', 'rep'))]
    dot_general x10 -> x0, matrix products: 24.9 us -> none  [the longest x1 8.95 us: body(): jnp.einsum('td,dcm->tcm', modulated, lax.all_gather(w_qkv, 'rep', axis=0,...]
    pallas_call x0 -> x7, Pallas kernels: none -> 24.7 us  [the longest x1 11 us: body(): call(first_kernel, 'first', [shape((rows, half), BF16), shape((3, rows, w...]
    dot_general x5 -> x0, local copies, waits for them, and re-layouts: 21.2 us -> none  [the longest x2 19.3 us: body(): jnp.einsum('td,dcm->tcm', modulated, lax.all_gather(w_qkv, 'rep', axis=0,...]
    ppermute x0 -> x12, starting transfers between devices: none -> 10.5 us  [the longest x5 8.73 us: shift(): lax.ppermute(value, axis, [(i, (i + by) % size) for i in range(size)])]
    ppermute x0 -> x12, waiting for transfers between devices: none -> 7.73 us  [the longest x5 6.5 us: shift(): lax.ppermute(value, axis, [(i, (i + by) % size) for i in range(size)])]
  transfers between devices with their start and end apart: 4 -> 12, of which waited for: 4 -> 6; matrix products, arithmetic and copies ran while one was open for 19% -> 0% of each run, Pallas kernels for 0% -> 40%
where the time goes in v1:
time: 45.2 us; the launch traced here: 45 us
  Pallas kernels  24.7 us (55%)
  starting transfers between devices  10.5 us (23%)
  waiting for transfers between devices  7.73 us (17%)
  local copies, waits for them, and re-layouts  2.13 us (5%)
    pallas_call x1, Pallas kernels, body(): call(first_kernel, 'first', [shape((rows, half), BF16), shape((3, rows, w...  11 us
    ppermute x5, starting transfers between devices, shift(): lax.ppermute(value, axis, [(i, (i + by) % size) for i in range(size)])  8.73 us
    ppermute x5, waiting for transfers between devices, shift(): lax.ppermute(value, axis, [(i, (i + by) % size) for i in range(size)])  6.5 us
    pallas_call x1, Pallas kernels, body(): call(load_kernel, 'load', shape((2, half, width), BF16), [HB], scratch=[d...  3.55 us
    pallas_call x1, Pallas kernels, body(): call(functools.partial(sixth_kernel, mp - 1, mp, tiles), 'others', shape(...  3.03 us
    pallas_call x1, Pallas kernels, body(): call(fifth_kernel, 'own', [shape((cols, rows), F32), shape((cols, tiles *...  2.83 us
    pallas_call x1, Pallas kernels, body(): call(second_kernel, 'second', shape(block, BF16), [HB, VM, VM, VM], scrat...  2.61 us
    unnamed x12, local copies, waits for them, and re-layouts  2.13 us
  transfers between devices with their start and end apart: 12, of which 6 were waited for; matrix products, arithmetic and copies ran while one was open for 0% of the time, Pallas kernels for 40%

profile of v1, /device:TPU:0, one launch (start us, length us, event | category | flops | bytes accessed | tf_op | source)
XLA Modules:
  0.0 45.0 jit_solution(175184184748166787)
XLA Ops:
  0.0 3.6 %load.1.kv_ref = bf16[2,1120,640]{2,1,0:T(8,128)(2,1)} custom-call(bf16[3,1120,640]{2,1,0:T(8,128)(2,1)} %bitcast.9), custom_call_target="tpu_custom_call" | custom-call | bytes 2867200 | tf_op jit(solution)/shard_map/load/pallas_call | solution.py:300
  3.6 0.6 %collective-permute-start.1 = (bf16[2,1120,640]{2,1,0:T(8,128)(2,1)}, bf16[2,1120,640]{2,1,0:T(8,128)(2,1)S(1)}, u32[]{:S(2)}, u32[]{:S(2)}) collective-permute-start(bf16[2,1120,640]{2,1,0:T(8,128)(2,1)} %load.1.kv_ref), channel_id=1, source_target_pairs={{0,1},{1,0},{2,3},{3,2},{4,5},{5,4},{6,7},{7,6},{8,9},{9,8},{10,11... | collective-permute-start | bytes 8601608 | tf_op jit(solution)/shard_map/ppermute | solution.py:298
  4.1 11.0 %first.1 = (bf16[512,1120]{1,0:T(8,128)(2,1)S(1)}, f32[3,512,640]{2,1,0:T(8,128)}, bf16[1120,640]{1,0:T(8,128)(2,1)S(1)}) custom-call(s32[2]{0:T(128)S(1)} %copy-done.5, bf16[2240,512]{1,0:T(8,128)(2,1)S(1)} %bitcast.4, f32[6,3,2240]{2,1,0:T(4,128)S(1)} %copy-done.4, bf16[3,1120,640]{2,1,0:T(8,128)(2,1)} %bitcast.10, bf16[2,1120,640]{2,1,0:T(8,128)(2,1)} %load.1.kv_ref), custom_call_target="tpu_custom_call" | custom-call | flops 2202009600 | bytes 12582912 | tf_op jit(solution)/shard_map/first/pallas_call | solution.py:303
  15.2 0.1 collective-permute-start
  15.3 0.5 %collective-permute-start.11 = (bf16[1120,640]{1,0:T(8,128)(2,1)S(1)}, bf16[1120,640]{1,0:T(8,128)(2,1)S(1)}, u32[]{:S(2)}, u32[]{:S(2)}) collective-permute-start(bf16[1120,640]{1,0:T(8,128)(2,1)S(1)} %bitcast.6), channel_id=1, source_target_pairs={{0,1},{1,0},{2,3},{3,2},{4,5},{5,4},{6,7},{7,6},{8,9},{9,8},{10,11... | collective-permute-start | bytes 4300808 | tf_op jit(solution)/shard_map/ppermute | solution.py:298
  15.8 2.1 %copy-done = f32[3,512,640]{2,1,0:T(8,128)S(1)} copy-done((f32[3,512,640]{2,1,0:T(8,128)S(1)}, f32[3,512,640]{2,1,0:T(8,128)}, u32[]{:S(2)}) %copy-start) | copy-done | bytes 3932184
  17.9 2.6 %second.1.after_ref.refs_0_ = bf16[72,640]{1,0:T(8,128)(2,1)S(1)} custom-call(s32[2]{0:T(128)S(1)} %copy-done.5, bf16[512,1120]{1,0:T(8,128)(2,1)S(1)} %get-tuple-element.12.mod_ref, bf16[2,1120,640]{2,1,0:T(8,128)(2,1)S(1)} %collective-permute-done.1.w_ref, f32[3,512,640]{2,1,0:T(8,128)S(1)} %copy-done), custom_call_target="tpu_custom_call" | custom-call | flops 1468006400 | bytes 8388608 | tf_op jit(solution)/shard_map/second/pallas_call | solution.py:315
  20.5 1.2 %query.1.q_ref = bf16[512,640]{1,0:T(8,128)(2,1)S(1)} custom-call(bf16[512,1120]{1,0:T(8,128)(2,1)S(1)} %get-tuple-element.12.mod_ref, bf16[1120,640]{1,0:T(8,128)(2,1)S(1)} %collective-permute-done.w_ref, f32[3,512,640]{2,1,0:T(8,128)S(1)} %copy-done.1, bf16[72,640]{1,0:T(8,128)(2,1)S(1)} %second.1.after_ref.refs_0_), custom_call_target="tpu_custom_call" | custom-call | flops 734003200 | bytes 4194304 | tf_op jit(solution)/shard_map/query/pallas_call | solution.py:321
  21.7 2.6 %collective-permute-start.2 = (bf16[512,640]{1,0:T(8,128)(2,1)S(1)}, bf16[512,640]{1,0:T(8,128)(2,1)S(1)}, u32[]{:S(2)}, u32[]{:S(2)}) collective-permute-start(bf16[512,640]{1,0:T(8,128)(2,1)S(1)} %query.1.q_ref), channel_id=1, source_target_pairs={{0,2},{2,0},{1,3},{3,1},{4,6},{6,4},{5,7},{7,5},{8,10},{10,8},{9,1... | collective-permute-start | bytes 1966088 | tf_op jit(solution)/shard_map/ppermute | solution.py:295
  24.3 1.6 %collective-permute-start.3 = (bf16[72,640]{1,0:T(8,128)(2,1)S(1)}, bf16[72,640]{1,0:T(8,128)(2,1)S(1)}, u32[]{:S(2)}, u32[]{:S(2)}) collective-permute-start(bf16[72,640]{1,0:T(8,128)(2,1)S(1)} %second.1.after_ref.refs_0_), channel_id=1, source_target_pairs={{0,4},{4,8},{8,12},{12,0},{1,5},{5,9},{9,13},{13,1},{2,6},{6,10},{... | collective-permute-start | bytes 276488 | tf_op jit(solution)/shard_map/ppermute | solution.py:295
  25.9 2.6 %collective-permute-start.4 = (bf16[72,640]{1,0:T(8,128)(2,1)S(1)}, bf16[72,640]{1,0:T(8,128)(2,1)S(1)}, u32[]{:S(2)}, u32[]{:S(2)}) collective-permute-start(bf16[72,640]{1,0:T(8,128)(2,1)S(1)} %second.1.after_ref.refs_0_), channel_id=1, source_target_pairs={{0,8},{4,12},{8,0},{12,4},{1,9},{5,13},{9,1},{13,5},{2,10},{6,14},... | collective-permute-start | bytes 276488 | tf_op jit(solution)/shard_map/ppermute | solution.py:295
  28.5 1.3 %collective-permute-start.5 = (bf16[72,640]{1,0:T(8,128)(2,1)S(1)}, bf16[72,640]{1,0:T(8,128)(2,1)S(1)}, u32[]{:S(2)}, u32[]{:S(2)}) collective-permute-start(bf16[72,640]{1,0:T(8,128)(2,1)S(1)} %second.1.after_ref.refs_0_), channel_id=1, source_target_pairs={{0,12},{4,0},{8,4},{12,8},{1,13},{5,1},{9,5},{13,9},{2,14},{6,2},{... | collective-permute-start | bytes 276488 | tf_op jit(solution)/shard_map/ppermute | solution.py:295
  29.8 1.8 %collective-permute-done.3.refs_1_ = bf16[72,640]{1,0:T(8,128)(2,1)S(1)} collective-permute-done((bf16[72,640]{1,0:T(8,128)(2,1)S(1)}, bf16[72,640]{1,0:T(8,128)(2,1)S(1)}, u32[]{:S(2)}, u32[]{:S(2)}) %collective-permute-start.3) | collective-permute-done | bytes 92192 | tf_op jit(solution)/shard_map/ppermute | solution.py:295
  31.6 3.4 %collective-permute-done.4.refs_2_ = bf16[72,640]{1,0:T(8,128)(2,1)S(1)} collective-permute-done((bf16[72,640]{1,0:T(8,128)(2,1)S(1)}, bf16[72,640]{1,0:T(8,128)(2,1)S(1)}, u32[]{:S(2)}, u32[]{:S(2)}) %collective-permute-start.4) | collective-permute-done | bytes 92192 | tf_op jit(solution)/shard_map/ppermute | solution.py:295
  35.0 0.5 %collective-permute-start.8 = (bf16[72,640]{1,0:T(8,128)(2,1)S(1)}, bf16[72,640]{1,0:T(8,128)(2,1)S(1)}, u32[]{:S(2)}, u32[]{:S(2)}) collective-permute-start(bf16[72,640]{1,0:T(8,128)(2,1)S(1)} %collective-permute-done.4.refs_2_), channel_id=1, source_target_pairs={{0,1},{1,0},{2,3},{3,2},{4,5},{5,4},{6,7},{7,6},{8,9},{9,8},{10,11... | collective-permute-start | bytes 276488 | tf_op jit(solution)/shard_map/ppermute | solution.py:298
  35.5 0.1 collective-permute-start.9
  35.6 0.7 %collective-permute-done.7.refs_5_ = bf16[72,640]{1,0:T(8,128)(2,1)S(1)} collective-permute-done((bf16[72,640]{1,0:T(8,128)(2,1)S(1)}, bf16[72,640]{1,0:T(8,128)(2,1)S(1)}, u32[]{:S(2)}, u32[]{:S(2)}) %collective-permute-start.7) | collective-permute-done | bytes 92192 | tf_op jit(solution)/shard_map/ppermute | solution.py:298
  36.3 0.2 collective-permute-done.8.refs_6_
  36.4 0.4 collective-permute-done.9.refs_7_
  36.8 0.4 sum.1
  37.2 0.6 %collective-permute-start.10 = (bf16[72,640]{1,0:T(8,128)(2,1)S(1)}, bf16[72,640]{1,0:T(8,128)(2,1)S(1)}, u32[]{:S(2)}, u32[]{:S(2)}) collective-permute-start(bf16[72,640]{1,0:T(8,128)(2,1)S(1)} %get-tuple-element.15), channel_id=1, source_target_pairs={{0,2},{2,0},{1,3},{3,1},{4,6},{6,4},{5,7},{7,5},{8,10},{10,8},{9,1... | collective-permute-start | bytes 276488 | tf_op jit(solution)/shard_map/ppermute | solution.py:295
  37.8 2.8 %own.1 = (f32[1120,512]{1,0:T(8,128)S(1)}, f32[1120,256]{1,0:T(8,128)S(1)}) custom-call(s32[2]{0:T(128)S(1)} %copy-done.5, bf16[512,640]{1,0:T(8,128)(2,1)S(1)} %query.1.q_ref, f32[72,640]{1,0:T(8,128)S(1)} %get-tuple-element.16.state_ref, bf16[1120,640]{1,0:T(8,128)(2,1)S(1)} %bitcast.7, bf16[1120,640]{1,0:T(8,128)(2,1)S(1)} %collective-permute-done.11.w1_ref.refs_3_, ...), custom_call_target="tpu_custom_call" | custom-call | flops 734003200 | bytes 4194304 | tf_op jit(solution)/shard_map/own/pallas_call | solution.py:332
  40.7 1.3 %collective-permute-done.10.refs_1_ = bf16[72,640]{1,0:T(8,128)(2,1)S(1)} collective-permute-done((bf16[72,640]{1,0:T(8,128)(2,1)S(1)}, bf16[72,640]{1,0:T(8,128)(2,1)S(1)}, u32[]{:S(2)}, u32[]{:S(2)}) %collective-permute-start.10) | collective-permute-done | bytes 92192 | tf_op jit(solution)/shard_map/ppermute | solution.py:295
  42.0 3.0 %others.1 = bf16[1120,512]{1,0:T(8,128)(2,1)} custom-call(bf16[512,640]{1,0:T(8,128)(2,1)S(1)} %collective-permute-done.2.refs_0_, bf16[72,640]{1,0:T(8,128)(2,1)S(1)} %collective-permute-done.10.refs_1_, bf16[1120,640]{1,0:T(8,128)(2,1)S(1)} %bitcast.8, bf16[1120,640]{1,0:T(8,128)(2,1)S(1)} %collective-permute-done.11.w1_ref.refs_3_, ...), custom_call_target="tpu_custom_call" | custom-call | flops 734003200 | bytes 4194304 | tf_op jit(solution)/shard_map/others/pallas_call | solution.py:341
  (19 shorter events, 0.0 us)
Async XLA Ops:
  0.0 4.1 %copy-start.2 = (bf16[512,2240]{0,1:T(8,128)(2,1)S(1)}, bf16[512,2240]{0,1:T(8,128)(2,1)}, u32[]{:S(2)}) copy-start(bf16[512,2240]{0,1:T(8,128)(2,1)} %param.5) | copy-start | bytes 6881284
  0.0 4.1 %copy-start.4 = (f32[6,3,2240]{2,1,0:T(4,128)S(1)}, f32[6,3,2240]{2,1,0:T(4,128)}, u32[]{:S(2)}) copy-start(f32[6,3,2240]{2,1,0:T(4,128)} %mods_ref.3) | copy-start | bytes 483844
  0.0 4.1 %copy-start.5 = (s32[2]{0:T(128)S(1)}, s32[2]{0:T(128)}, u32[]{:S(2)}) copy-start(s32[2]{0:T(128)} %img_ref.5) | copy-start | bytes 28
  3.6 12.2 %collective-permute-start.1 = (bf16[2,1120,640]{2,1,0:T(8,128)(2,1)}, bf16[2,1120,640]{2,1,0:T(8,128)(2,1)S(1)}, u32[]{:S(2)}, u32[]{:S(2)}) collective-permute-start(bf16[2,1120,640]{2,1,0:T(8,128)(2,1)} %load.1.kv_ref), channel_id=1, source_target_pairs={{0,1},{1,0},{2,3},{3,2},{4,5},{5,4},{6,7},{7,6},{8,9},{9,8},{10,11... | collective-permute-start | bytes 8601608 | tf_op jit(solution)/shard_map/ppermute | solution.py:298
  4.1 11.1 %copy-start.3 = (bf16[640,1120]{0,1:T(8,128)(2,1)S(1)}, bf16[640,1120]{0,1:T(8,128)(2,1)}, u32[]{:S(2)}) copy-start(bf16[640,1120]{0,1:T(8,128)(2,1)} %param.9) | copy-start | bytes 4300804
  15.2 5.3 %collective-permute-start = (bf16[1120,640]{1,0:T(8,128)(2,1)S(1)}, bf16[1120,640]{1,0:T(8,128)(2,1)S(1)}, u32[]{:S(2)}, u32[]{:S(2)}) collective-permute-start(bf16[1120,640]{1,0:T(8,128)(2,1)S(1)} %get-tuple-element.13), channel_id=1, source_target_pairs={{0,1},{1,0},{2,3},{3,2},{4,5},{5,4},{6,7},{7,6},{8,9},{9,8},{10,11... | collective-permute-start | bytes 4300808 | tf_op jit(solution)/shard_map/ppermute | solution.py:298
  15.3 22.5 %collective-permute-start.11 = (bf16[1120,640]{1,0:T(8,128)(2,1)S(1)}, bf16[1120,640]{1,0:T(8,128)(2,1)S(1)}, u32[]{:S(2)}, u32[]{:S(2)}) collective-permute-start(bf16[1120,640]{1,0:T(8,128)(2,1)S(1)} %bitcast.6), channel_id=1, source_target_pairs={{0,1},{1,0},{2,3},{3,2},{4,5},{5,4},{6,7},{7,6},{8,9},{9,8},{10,11... | collective-permute-start | bytes 4300808 | tf_op jit(solution)/shard_map/ppermute | solution.py:298
  15.8 2.1 %copy-start = (f32[3,512,640]{2,1,0:T(8,128)S(1)}, f32[3,512,640]{2,1,0:T(8,128)}, u32[]{:S(2)}) copy-start(f32[3,512,640]{2,1,0:T(8,128)} %get-tuple-element.14.part_ref) | copy-start | bytes 11796484
  17.9 2.6 %copy-start.1 = (f32[3,512,640]{2,1,0:T(8,128)S(1)}, f32[3,512,640]{2,1,0:T(8,128)}, u32[]{:S(2)}) copy-start(f32[3,512,640]{2,1,0:T(8,128)} %get-tuple-element.14.part_ref) | copy-start | bytes 11796484
  21.7 20.3 %collective-permute-start.2 = (bf16[512,640]{1,0:T(8,128)(2,1)S(1)}, bf16[512,640]{1,0:T(8,128)(2,1)S(1)}, u32[]{:S(2)}, u32[]{:S(2)}) collective-permute-start(bf16[512,640]{1,0:T(8,128)(2,1)S(1)} %query.1.q_ref), channel_id=1, source_target_pairs={{0,2},{2,0},{1,3},{3,1},{4,6},{6,4},{5,7},{7,5},{8,10},{10,8},{9,1... | collective-permute-start | bytes 1966088 | tf_op jit(solution)/shard_map/ppermute | solution.py:295
  24.3 7.3 %collective-permute-start.3 = (bf16[72,640]{1,0:T(8,128)(2,1)S(1)}, bf16[72,640]{1,0:T(8,128)(2,1)S(1)}, u32[]{:S(2)}, u32[]{:S(2)}) collective-permute-start(bf16[72,640]{1,0:T(8,128)(2,1)S(1)} %second.1.after_ref.refs_0_), channel_id=1, source_target_pairs={{0,4},{4,8},{8,12},{12,0},{1,5},{5,9},{9,13},{13,1},{2,6},{6,10},{... | collective-permute-start | bytes 276488 | tf_op jit(solution)/shard_map/ppermute | solution.py:295
  25.9 9.1 %collective-permute-start.4 = (bf16[72,640]{1,0:T(8,128)(2,1)S(1)}, bf16[72,640]{1,0:T(8,128)(2,1)S(1)}, u32[]{:S(2)}, u32[]{:S(2)}) collective-permute-start(bf16[72,640]{1,0:T(8,128)(2,1)S(1)} %second.1.after_ref.refs_0_), channel_id=1, source_target_pairs={{0,8},{4,12},{8,0},{12,4},{1,9},{5,13},{9,1},{13,5},{2,10},{6,14},... | collective-permute-start | bytes 276488 | tf_op jit(solution)/shard_map/ppermute | solution.py:295
  28.5 6.5 %collective-permute-start.5 = (bf16[72,640]{1,0:T(8,128)(2,1)S(1)}, bf16[72,640]{1,0:T(8,128)(2,1)S(1)}, u32[]{:S(2)}, u32[]{:S(2)}) collective-permute-start(bf16[72,640]{1,0:T(8,128)(2,1)S(1)} %second.1.after_ref.refs_0_), channel_id=1, source_target_pairs={{0,12},{4,0},{8,4},{12,8},{1,13},{5,1},{9,5},{13,9},{2,14},{6,2},{... | collective-permute-start | bytes 276488 | tf_op jit(solution)/shard_map/ppermute | solution.py:295
  31.6 3.9 %collective-permute-start.6 = (bf16[72,640]{1,0:T(8,128)(2,1)S(1)}, bf16[72,640]{1,0:T(8,128)(2,1)S(1)}, u32[]{:S(2)}, u32[]{:S(2)}) collective-permute-start(bf16[72,640]{1,0:T(8,128)(2,1)S(1)} %second.1.after_ref.refs_0_), channel_id=1, source_target_pairs={{0,1},{1,0},{2,3},{3,2},{4,5},{5,4},{6,7},{7,6},{8,9},{9,8},{10,11... | collective-permute-start | bytes 276488 | tf_op jit(solution)/shard_map/ppermute | solution.py:298
  35.0 1.3 %collective-permute-start.7 = (bf16[72,640]{1,0:T(8,128)(2,1)S(1)}, bf16[72,640]{1,0:T(8,128)(2,1)S(1)}, u32[]{:S(2)}, u32[]{:S(2)}) collective-permute-start(bf16[72,640]{1,0:T(8,128)(2,1)S(1)} %collective-permute-done.3.refs_1_), channel_id=1, source_target_pairs={{0,1},{1,0},{2,3},{3,2},{4,5},{5,4},{6,7},{7,6},{8,9},{9,8},{10,11... | collective-permute-start | bytes 276488 | tf_op jit(solution)/shard_map/ppermute | solution.py:298
  35.0 1.4 %collective-permute-start.8 = (bf16[72,640]{1,0:T(8,128)(2,1)S(1)}, bf16[72,640]{1,0:T(8,128)(2,1)S(1)}, u32[]{:S(2)}, u32[]{:S(2)}) collective-permute-start(bf16[72,640]{1,0:T(8,128)(2,1)S(1)} %collective-permute-done.4.refs_2_), channel_id=1, source_target_pairs={{0,1},{1,0},{2,3},{3,2},{4,5},{5,4},{6,7},{7,6},{8,9},{9,8},{10,11... | collective-permute-start | bytes 276488 | tf_op jit(solution)/shard_map/ppermute | solution.py:298
  35.5 1.3 %collective-permute-start.9 = (bf16[72,640]{1,0:T(8,128)(2,1)S(1)}, bf16[72,640]{1,0:T(8,128)(2,1)S(1)}, u32[]{:S(2)}, u32[]{:S(2)}) collective-permute-start(bf16[72,640]{1,0:T(8,128)(2,1)S(1)} %collective-permute-done.5.refs_3_), channel_id=1, source_target_pairs={{0,1},{1,0},{2,3},{3,2},{4,5},{5,4},{6,7},{7,6},{8,9},{9,8},{10,11... | collective-permute-start | bytes 276488 | tf_op jit(solution)/shard_map/ppermute | solution.py:298
  37.2 4.8 %collective-permute-start.10 = (bf16[72,640]{1,0:T(8,128)(2,1)S(1)}, bf16[72,640]{1,0:T(8,128)(2,1)S(1)}, u32[]{:S(2)}, u32[]{:S(2)}) collective-permute-start(bf16[72,640]{1,0:T(8,128)(2,1)S(1)} %get-tuple-element.15), channel_id=1, source_target_pairs={{0,2},{2,0},{1,3},{3,1},{4,6},{6,4},{5,7},{7,5},{8,10},{10,8},{9,1... | collective-permute-start | bytes 276488 | tf_op jit(solution)/shard_map/ppermute | solution.py:295
